TPU v7x, 32 devices: a whole 2x2x4 slice. The times are simulated.
32 devices in a mesh: grp: 2 (over y), freq: 4 (over z), tm: 2 (over x), pol: 2 (over core).
Axes of the slice: x: 2, y: 2, z: 4, core: 2. Of those that a mesh axis runs over, the one named last changes fastest.
Arguments:
- voltages: bfloat16 [2, 8, 1024, 4, 2, 256], P('pol', ('grp', 'freq'), 'tm'), parts along dimension 1, may hold values from -6 to 6
- feed_gains: float32 [8, 2, 4, 2, 256], P(('grp', 'freq'), 'pol'), parts along dimension 0, may hold values from -5 to 5
- owner_table: int32 [64], replicated, may hold values from 0 to 3, as said below
- keep_flags: int32 [1024], replicated, may hold values 0 or 1
Outputs:
- owned: bfloat16 [128, 64, 2048], P(('grp', 'tm', 'pol'), None, 'freq'), parts along dimension 0
There are 2 independent parts, one for each index of `grp`. A program takes and returns all parts, laid end to end along the dimension named above; an argument that names none is the same for every part. Nothing has to cross between parts.
Inputs may be any that keep to these rules, and one draw needn't show every extreme that they name: `owner_table`: each index of freq owns from 0 to 32 beam sets; one owns exactly 32.
All inputs are finite; a program needn't handle non-finite values.
Results may differ from a plain program's by a relative error of at most 0.0058.
Values may be sent and summed in bfloat16 or wider, within the bound.
No kernel may reach another device: no remote copies, remote signals or barrier semaphores. Data moves between devices by JAX's collectives and lax.ppermute only.
A program may use at most 64 MiB of HBM per device.

v0:
```python
import jax
import jax.numpy as jnp
from jax import lax
from jax.sharding import PartitionSpec as P

NS = 256
CYL = 4
UPCH = 16
TAPS = 16
SET_BEAMS = 16


def shifted(block, axis, distance):
    devices = range(lax.axis_size(axis))
    route = [(i - distance, i) for i in devices if i - distance in devices]
    return lax.ppermute(block, axis, route)


def window_taps():
    span = TAPS * UPCH
    steps = jnp.arange(span, dtype=jnp.float32)
    weights = (
        jnp.sinc((steps - (span - 1) / 2.0) / UPCH) * jnp.sin(jnp.pi * (steps + 0.5) / span) ** 2
    )
    weights = weights / jnp.sqrt(jnp.sum(weights * weights))
    return weights.reshape(TAPS, UPCH)


def fine_tables():
    rows = jnp.arange(UPCH, dtype=jnp.int32)
    phase = rows[:, None] * rows[None, :] % UPCH
    angle = 2.0 * jnp.pi * phase.astype(jnp.float32) / UPCH
    return (jnp.cos(angle), jnp.sin(angle))


def beam_matrix():
    rows = jnp.arange(NS, dtype=jnp.int32)
    phase = rows[:, None] * rows[None, :] % NS
    angle = 2.0 * jnp.pi * phase.astype(jnp.float32) / NS
    scale = 1.0 / jnp.sqrt(jnp.float32(NS))
    cosine = jnp.cos(angle) * scale
    sine = jnp.sin(angle) * scale
    upper = jnp.concatenate([cosine, -sine], axis=1)
    lower = jnp.concatenate([sine, cosine], axis=1)
    return jnp.concatenate([upper, lower], axis=0).astype(jnp.bfloat16)


def cylinder_tables():
    rows = jnp.arange(CYL, dtype=jnp.int32)
    phase = rows[:, None] * rows[None, :] % CYL
    angle = 2.0 * jnp.pi * phase.astype(jnp.float32) / CYL
    return (0.5 * jnp.cos(angle), 0.5 * jnp.sin(angle))


def power_frames(frames, gain_pol, n_out):
    window = window_taps()
    fine_cos, fine_sin = fine_tables()
    beam_table = beam_matrix()
    cyl_cos, cyl_sin = cylinder_tables()
    highest = lax.Precision.HIGHEST
    chan_count = frames.shape[0]
    summed = jnp.zeros((chan_count, n_out) + frames.shape[2:], jnp.float32)
    for tap_index in range(TAPS):
        weights = window[tap_index].reshape(1, 1, UPCH, 1, 1, 1)
        summed = summed + weights * frames[:, tap_index : tap_index + n_out].astype(jnp.float32)
    real_part = summed[:, :, :, :, 0, :]
    imag_part = summed[:, :, :, :, 1, :]
    spec_real = jnp.einsum("qk,cmkxn->mcqxn", fine_cos, real_part, precision=highest) + jnp.einsum(
        "qk,cmkxn->mcqxn", fine_sin, imag_part, precision=highest
    )
    spec_imag = jnp.einsum("qk,cmkxn->mcqxn", fine_cos, imag_part, precision=highest) - jnp.einsum(
        "qk,cmkxn->mcqxn", fine_sin, real_part, precision=highest
    )
    gain_real = gain_pol[:, :, 0, :][None, :, None]
    gain_imag = gain_pol[:, :, 1, :][None, :, None]
    cal_real = spec_real * gain_real - spec_imag * gain_imag
    cal_imag = spec_real * gain_imag + spec_imag * gain_real
    calibrated = jnp.stack([cal_real, cal_imag], axis=4).astype(jnp.bfloat16)
    row_count = n_out * chan_count * UPCH
    flat = calibrated.reshape(row_count * CYL, 2 * NS)
    partial_value = jnp.dot(flat, beam_table, preferred_element_type=jnp.float32)
    partial_value = partial_value.reshape(row_count, CYL, 2, NS)
    beam_real = partial_value[:, :, 0, :]
    beam_imag = partial_value[:, :, 1, :]
    form_real = jnp.einsum("ec,rcn->ren", cyl_cos, beam_real, precision=highest) + jnp.einsum(
        "ec,rcn->ren", cyl_sin, beam_imag, precision=highest
    )
    form_imag = jnp.einsum("ec,rcn->ren", cyl_cos, beam_imag, precision=highest) - jnp.einsum(
        "ec,rcn->ren", cyl_sin, beam_real, precision=highest
    )
    powers = (form_real * form_real + form_imag * form_imag).astype(jnp.bfloat16)
    return powers.reshape(n_out, chan_count * UPCH, CYL * NS)


def slot_columns(owner_table, keep_flags, n_owner, most_sets):
    count = owner_table.shape[0]
    order = jnp.arange(count, dtype=jnp.int32)
    same_owner = owner_table[:, None] == owner_table[None, :]
    earlier = order[None, :] < order[:, None]
    set_rank = jnp.sum(jnp.logical_and(same_owner, earlier).astype(jnp.int32), axis=1)
    slot_index = owner_table * most_sets + set_rank
    places = jnp.arange(n_owner * most_sets, dtype=jnp.int32)
    matches = (slot_index[None, :] == places[:, None]).astype(jnp.int32)
    filled = jnp.sum(matches, axis=1)
    set_of = jnp.sum(matches * order[None, :], axis=1)
    within = jnp.arange(SET_BEAMS, dtype=jnp.int32)
    beam_index = (set_of[:, None] * SET_BEAMS + within[None, :]).reshape(-1)
    kept = jnp.take(keep_flags, beam_index).reshape(-1, SET_BEAMS)
    column_mask = (filled[:, None] * kept).reshape(-1)
    return (beam_index, column_mask)


def per_device(voltages, feed_gains, owner_table, keep_flags):
    samples = voltages[0]
    chan_count = samples.shape[0]
    frame_count = samples.shape[1] // UPCH
    frames = samples.reshape(chan_count, frame_count, UPCH, CYL, 2, NS)
    gain_pol = feed_gains[:, 0]
    history = TAPS - 1
    tail_frames = frames[:, frame_count - history :]
    before = shifted(tail_frames, "tm", 1)
    joined = jnp.concatenate([before, frames], axis=1)
    powers = power_frames(joined, gain_pol, frame_count)
    n_owner = lax.axis_size("freq")
    most_sets = 2 * owner_table.shape[0] // n_owner
    beam_index, column_mask = slot_columns(owner_table, keep_flags, n_owner, most_sets)
    mask_values = column_mask.astype(jnp.bfloat16)[None, None, :]
    summed = (
        lax.psum_scatter(powers, "pol", scatter_dimension=0, tiled=True)
        .astype(jnp.float32)
        .astype(jnp.bfloat16)
    )
    outgoing = jnp.take(summed, beam_index, axis=2) * mask_values
    return lax.all_to_all(outgoing, "freq", split_axis=2, concat_axis=1, tiled=True)


def solution(mesh):
    return jax.shard_map(
        per_device,
        mesh=mesh,
        in_specs=(
            P("pol", ("grp", "freq"), "tm", None, None, None),
            P(("grp", "freq"), "pol", None, None, None),
            P(),
            P(),
        ),
        out_specs=P(("grp", "tm", "pol"), None, "freq"),
        check_vma=False,
    )
```

profile of v0, /device:TPU:0, one launch (start us, length us, event | category | flops | bytes accessed | tf_op | source)
XLA Modules:
  0.0 210.3 jit_solution(8894756028634160894)
XLA Ops:
  6.5 2.0 copy.21
  9.7 5.8 %collective-permute-start = (bf16[1,15,16,4,2,256]{5,2,3,1,4,0:T(8,128)(2,1)}, bf16[1,15,16,4,2,256]{5,2,3,1,4,0:T(8,128)(2,1)}, u32[]{:S(2)}, u32[]{:S(2)}) collective-permute-start(bf16[1,15,16,4,2,256]{5,2,3,1,4,0:T(8,128)(2,1)} %copy.53), channel_id=1, source_target_pairs={{0,2},{1,3},{4,6},{5,7},{8,10},{9,11},{12,14},{13,15},{16,18},{17,... | collective-permute-start | bytes 2949128 | tf_op jit(solution)/shard_map/ppermute | solution.py:16
  19.1 16.8 %collective-permute-done = bf16[1,15,16,4,2,256]{5,2,3,1,4,0:T(8,128)(2,1)} collective-permute-done((bf16[1,15,16,4,2,256]{5,2,3,1,4,0:T(8,128)(2,1)}, bf16[1,15,16,4,2,256]{5,2,3,1,4,0:T(8,128)(2,1)}, u32[]{:S(2)}, u32[]{:S(2)}) %collective-permute-start) | collective-permute-done | bytes 983072 | tf_op jit(solution)/shard_map/ppermute | solution.py:16
  35.9 1.3 constant_dynamic-update-slice_fusion.1
  37.5 8.6 %multiply_add_fusion = f32[1,32,16,4,2,256]{5,2,3,1,4,0:T(8,128)S(1)} fusion(bf16[1,47,16,4,2,256]{5,2,3,1,4,0:T(8,128)(2,1)S(1)} %constant_dynamic-update-slice_fusion, f32[16]{0:T(128)S(1)} %get-tuple-element.16, f32[16]{0:T(128)S(1)} %get-tuple-element.17, f32[16]{0:T(128)S(1)} %get-tuple-element.18, f32[16]{0:T(128)S(1)} %get-tuple-element.19, ...), kind=kLoop, calls=%fused_computation.3 | loop fusion | flops 49283072 | bytes 37749760 | tf_op jit(solution)/shard_map/add | solution.py:65
  46.1 2.0 fusion.6
  48.1 1.9 fusion.9
  50.0 2.0 fusion.21
  52.0 2.6 %fusion.26 = (bf16[32,1,16,4,1,256]{5,2,3,0,4,1:T(8,128)(2,1)S(1)}, bf16[32,1,16,4,1,256]{5,2,3,0,4,1:T(8,128)(2,1)S(1)}) fusion(f32[32,4,256,16]{2,3,1,0:T(8,128)S(1)} %fusion.21, f32[4,256]{1,0:T(4,128)S(1)} %get-tuple-element.33, f32[4,256]{1,0:T(4,128)S(1)} %get-tuple-element.34, f32[32,4,256,16]{2,3,1,0:T(8,128)S(1)} %fusion.6, ...), kind=kOutput, calls=%fused_computation.36 | convolution fusion | flops 105385472 | bytes 8396800 | tf_op jit(solution)/shard_map/qk,cmkxn->mcqxn/dot_general | solution.py:71
  54.9 4.8 %copy.25 = bf16[32,1,16,4,2,256]{5,4,2,0,3,1:T(2,128)(2,1)} copy(bf16[32,1,16,4,2,256]{5,2,3,0,4,1:T(8,128)(2,1)S(1)} %pad_maximum_fusion) | data formatting | bytes 4194304 | tf_op jit(solution)/shard_map/stack | solution.py:78
  59.7 3.2 %reshape.273 = bf16[512,4,512,1]{2,0,1,3:T(8,128)(2,1)S(1)} reshape(bf16[32,1,16,4,2,256]{5,4,2,0,3,1:T(2,128)(2,1)} %copy.25) | data formatting | bytes 4194304 | tf_op jit(solution)/shard_map/convert_element_type | solution.py:78
  64.4 4.4 %fusion.10 = f32[512,256,4]{1,2,0:T(4,128)S(1)} fusion(f32[512,4,256]{2,0,1:T(8,128)S(1)} %get-tuple-element.12), kind=kOutput, calls=%fused_computation.24 | convolution fusion | flops 25166064 | bytes 4194304 | tf_op jit(solution)/shard_map/ec,rcn->ren/dot_general | solution.py:88
  68.8 4.4 %fusion.12 = f32[512,256,4]{1,2,0:T(4,128)S(1)} fusion(f32[512,4,256]{2,0,1:T(8,128)S(1)} %get-tuple-element.12), kind=kOutput, calls=%fused_computation.26 | convolution fusion | flops 25166064 | bytes 4194304 | tf_op jit(solution)/shard_map/ec,rcn->ren/dot_general | solution.py:85
  73.2 4.4 %fusion.14 = f32[512,256,4]{1,2,0:T(4,128)S(1)} fusion(f32[512,4,256]{2,0,1:T(8,128)S(1)} %get-tuple-element.11), kind=kOutput, calls=%fused_computation.28 | convolution fusion | flops 25166064 | bytes 4194304 | tf_op jit(solution)/shard_map/ec,rcn->ren/dot_general | solution.py:88
  77.6 5.5 %fusion.22 = bf16[512,4,256]{2,1,0:T(4,128)(2,1)S(1)} fusion(f32[512,256,4]{1,2,0:T(4,128)S(1)} %fusion.10, f32[512,256,4]{1,2,0:T(4,128)S(1)} %fusion.14, f32[512,256,4]{1,2,0:T(4,128)S(1)} %fusion.12, f32[512,4,256]{2,0,1:T(8,128)S(1)} %get-tuple-element.11), kind=kOutput, calls=%fused_computation.34 | convolution fusion | flops 28311792 | bytes 9437184 | tf_op jit(solution)/shard_map/ec,rcn->ren/dot_general | solution.py:85
  83.9 12.3 %copy.30 = bf16[32,16,1024]{1,0,2:T(8,128)(2,1)} copy(bf16[32,16,1024]{2,1,0:T(8,128)(2,1)S(1)} %reshape.254) | data formatting | bytes 2097152 | tf_op jit(solution)/shard_map/reshape | solution.py:92
  97.6 8.6 %gather_fusion.1 = s32[2048]{0:T(1024)S(1)} fusion(s32[1024]{0:T(1024)S(1)} %copy-done, s32[2048]{0:T(1024)S(1)} %broadcast_clamp_fusion), kind=kCustom, calls=%fused_computation.1 | custom fusion | bytes 24576 | tf_op jit(solution)/shard_map/jit(_take)/gather | solution.py:108
  106.2 8.6 %reduce-scatter.2.cloned.1.call-done = bf16[16,16,1024]{1,0,2:T(8,128)(2,1)} async-done(((bf16[32,16,1024]{1,0,2:T(8,128)(2,1)}), bf16[16,16,1024]{1,0,2:T(8,128)(2,1)}) %reduce-scatter.2.cloned.1.call-update) | async-done | bytes 524304 | tf_op jit(solution)/shard_map/reduce_scatter | solution.py:129
  114.8 18.4 %gather_fusion = bf16[2048,16,16]{2,1,0:T(8,128)(2,1)} fusion(bf16[16,16,1024]{1,0,2:T(8,128)(2,1)} %reduce-scatter.2.cloned.1.call-done, s32[2048]{0:T(1024)S(1)} %broadcast_clamp_fusion), kind=kCustom, calls=%fused_computation | custom fusion | bytes 2105344 | tf_op jit(solution)/shard_map/jit(_take)/gather | solution.py:133
  133.2 13.1 %fusion.117 = bf16[2048,16,16]{2,1,0:T(8,128)(2,1)} fusion(bf16[2048]{0:T(1024)(128)(2,1)S(1)} %get-tuple-element.7, bf16[2048,16,16]{2,1,0:T(8,128)(2,1)} %gather_fusion, pred[2048]{0:T(1024)(128)(4,1)S(1)} %get-tuple-element.8), kind=kLoop, calls=%fused_computation.161 | loop fusion | flops 1048576 | bytes 2103296
  146.3 10.2 %reshape.278 = bf16[4,2,65536]{2,1,0:T(2,128)(2,1)S(1)} reshape(bf16[2048,16,16]{2,1,0:T(8,128)(2,1)} %fusion.117) | data formatting | bytes 2097152
  156.6 30.8 %all_to_all.18 = bf16[4,2,65536]{2,1,0:T(2,128)(2,1)S(1)} all-to-all(bf16[4,2,65536]{2,1,0:T(2,128)(2,1)S(1)} %reshape.278), channel_id=1, replica_groups=mesh['grp'=2,'freq'=4,'tm'=2,'pol'=2] {'freq'}, dimensions={0} | all-to-all | bytes 2097152 | tf_op jit(solution)/shard_map/all_to_all | solution.py:134
  187.4 6.9 %reshape.279 = bf16[2048,16,16]{2,1,0:T(8,128)(2,1)} reshape(bf16[4,2,65536]{2,1,0:T(2,128)(2,1)S(1)} %all_to_all.18) | data formatting | bytes 2097152
  194.3 9.1 %copy.31 = bf16[16,4,16,512]{3,2,1,0:T(8,128)(2,1)} copy(bf16[16,4,16,512]{2,0,3,1:T(8,128)(2,1)} %bitcast.109) | data formatting | bytes 2097152 | tf_op jit(solution)/shard_map/all_to_all | solution.py:134
  (35 shorter events, 8.3 us)
Async XLA Ops:
  6.5 91.0 %copy-start = (s32[1024]{0:T(1024)S(1)}, s32[1024]{0:T(1024)}, u32[]{:S(2)}) copy-start(s32[1024]{0:T(1024)} %param.7) | copy-start | bytes 12292
  6.5 108.3 %reduce-scatter.2.cloned.1.call-start = ((), (), s32[]{:S(2)}) async-start(), calls=%async_computation.2 | async-start | bytes 12582912 | tf_op jit(solution)/shard_map/reduce_scatter | solution.py:129
  8.6 10.5 %copy-start.1 = (f32[1,1,4,2,256]{4,3,2,1,0:T(2,128)S(1)}, f32[1,1,4,2,256]{4,3,2,1,0:T(2,128)}, u32[]{:S(2)}) copy-start(f32[1,1,4,2,256]{4,3,2,1,0:T(2,128)} %param.5) | copy-start | bytes 24580
  9.7 26.2 %collective-permute-start = (bf16[1,15,16,4,2,256]{5,2,3,1,4,0:T(8,128)(2,1)}, bf16[1,15,16,4,2,256]{5,2,3,1,4,0:T(8,128)(2,1)}, u32[]{:S(2)}, u32[]{:S(2)}) collective-permute-start(bf16[1,15,16,4,2,256]{5,2,3,1,4,0:T(8,128)(2,1)} %copy.53), channel_id=1, source_target_pairs={{0,2},{1,3},{4,6},{5,7},{8,10},{9,11},{12,14},{13,15},{16,18},{17,... | collective-permute-start | bytes 2949128 | tf_op jit(solution)/shard_map/ppermute | solution.py:16
  96.2 0.7 copy-start.2
Sparse Core Ops, SparseCore 0:
  96.3 18.4 reduce-scatter.1
where the time goes:
time: 211 us; the launch traced here: 210 us
  local copies, waits for them, and re-layouts  80.3 us (38%)
  blocking collectives  30.8 us (15%)
  matrix products  28.5 us (14%)
  waiting for transfers between devices  25.5 us (12%)
  other arithmetic  25.1 us (12%)
  between operations  14.3 us (7%)
  starting transfers between devices  5.82 us (3%)
    all_to_all x1, blocking collectives, per_device(): lax.all_to_all(outgoing, 'freq', split_axis=2, concat_axis=1, tiled=True)  30.8 us
    unnamed x12, local copies, waits for them, and re-layouts  22.2 us
    gather x1, local copies, waits for them, and re-layouts, per_device(): outgoing = jnp.take(summed, beam_index, axis=2) * mask_values  18.4 us
    ppermute x1, waiting for transfers between devices, shifted(): return lax.ppermute(block, axis, route)  16.8 us
    unnamed x1, other arithmetic  13.1 us
    reshape x2, local copies, waits for them, and re-layouts, power_frames(): return powers.reshape(n_out, chan_count * UPCH, CYL * NS)  13 us
    all_to_all x1, local copies, waits for them, and re-layouts, per_device(): lax.all_to_all(outgoing, 'freq', split_axis=2, concat_axis=1, tiled=True)  9.1 us
    reduce_scatter x1, waiting for transfers between devices, per_device(): lax.psum_scatter(powers, 'pol', scatter_dimension=0, tiled=True)  8.64 us
  transfers between devices with their start and end apart: 2, of which 2 were waited for; matrix products, arithmetic and copies ran while one was open for 6% of the time, Pallas kernels for 0%

commit v1 on v0

--- a/solution.py
+++ b/solution.py
@@ -131,7 +131,10 @@
         .astype(jnp.bfloat16)
     )
     outgoing = jnp.take(summed, beam_index, axis=2) * mask_values
-    return lax.all_to_all(outgoing, "freq", split_axis=2, concat_axis=1, tiled=True)
+    return jnp.concatenate(
+        lax.all_to_all(jnp.stack(jnp.split(outgoing, lax.axis_size("freq"), axis=2)), "freq", 0, 0),
+        axis=1,
+    )
 
 
 def solution(mesh):

time: 211 us -> 197 us (0.934)
  local copies, waits for them, and re-layouts: 80.3 us -> 67.1 us
    unnamed x12 -> x10, local copies, waits for them, and re-layouts: 22.2 us -> 5.02 us
    unnamed x1 -> x0, other arithmetic: 13.1 us -> none
    mul x0 -> x1, other arithmetic: none -> 12.3 us  [per_device(): outgoing = jnp.take(summed, beam_index, axis=2) * mask_values]
    another operation x0 -> x5, local copies, waits for them, and re-layouts: none -> 12 us  [per_device(): jnp.stack(jnp.split(outgoing, lax.axis_size('freq'), axis=2))]
    all_to_all x1, local copies, waits for them, and re-layouts: 9.1 us -> 1.06 us  [per_device(): lax.all_to_all(jnp.stack(jnp.split(outgoing, lax.axis_size('freq'), axis=...]
where the time goes in v1:
time: 197 us; the launch traced here: 196 us
  local copies, waits for them, and re-layouts  67.1 us (34%)
  blocking collectives  30.8 us (16%)
  matrix products  28.5 us (14%)
  waiting for transfers between devices  25.4 us (13%)
  other arithmetic  24.5 us (12%)
  between operations  14.3 us (7%)
  starting transfers between devices  5.83 us (3%)
    all_to_all x1, blocking collectives, per_device(): lax.all_to_all(jnp.stack(jnp.split(outgoing, lax.axis_size('freq'), axis=...  30.8 us
    gather x1, local copies, waits for them, and re-layouts, per_device(): outgoing = jnp.take(summed, beam_index, axis=2) * mask_values  18.3 us
    ppermute x1, waiting for transfers between devices, shifted(): return lax.ppermute(block, axis, route)  16.8 us
    reshape x2, local copies, waits for them, and re-layouts, power_frames(): return powers.reshape(n_out, chan_count * UPCH, CYL * NS)  13 us
    mul x1, other arithmetic, per_device(): outgoing = jnp.take(summed, beam_index, axis=2) * mask_values  12.3 us
    another operation x5, local copies, waits for them, and re-layouts, per_device(): jnp.stack(jnp.split(outgoing, lax.axis_size('freq'), axis=2))  12 us
    reduce_scatter x1, waiting for transfers between devices, per_device(): lax.psum_scatter(powers, 'pol', scatter_dimension=0, tiled=True)  8.64 us
    add x1, other arithmetic, power_frames(): summed + weights * frames[:, tap_index:tap_index + n_out].astype(jnp.floa...  8.6 us
  transfers between devices with their start and end apart: 2, of which 2 were waited for; matrix products, arithmetic and copies ran while one was open for 6% of the time, Pallas kernels for 0%

profile of v1, /device:TPU:0, one launch (start us, length us, event | category | flops | bytes accessed | tf_op | source)
XLA Modules:
  0.0 196.3 jit_solution(11209824515324255149)
XLA Ops:
  6.5 2.0 %copy.46 = bf16[1,1,512,4,2,256]{5,2,4,3,1,0:T(8,128)(2,1)S(1)} copy(bf16[1,1,512,4,2,256]{5,4,3,2,1,0:T(2,128)(2,1)} %param.4) | data formatting | bytes 4194304 | tf_op args[0]
  9.7 5.8 %collective-permute-start = (bf16[1,15,16,4,2,256]{5,2,3,1,4,0:T(8,128)(2,1)}, bf16[1,15,16,4,2,256]{5,2,3,1,4,0:T(8,128)(2,1)}, u32[]{:S(2)}, u32[]{:S(2)}) collective-permute-start(bf16[1,15,16,4,2,256]{5,2,3,1,4,0:T(8,128)(2,1)} %copy.82), channel_id=1, source_target_pairs={{0,2},{1,3},{4,6},{5,7},{8,10},{9,11},{12,14},{13,15},{16,18},{17,... | collective-permute-start | bytes 2949128 | tf_op jit(solution)/shard_map/ppermute | solution.py:16
  19.2 16.8 %collective-permute-done = bf16[1,15,16,4,2,256]{5,2,3,1,4,0:T(8,128)(2,1)} collective-permute-done((bf16[1,15,16,4,2,256]{5,2,3,1,4,0:T(8,128)(2,1)}, bf16[1,15,16,4,2,256]{5,2,3,1,4,0:T(8,128)(2,1)}, u32[]{:S(2)}, u32[]{:S(2)}) %collective-permute-start) | collective-permute-done | bytes 983072 | tf_op jit(solution)/shard_map/ppermute | solution.py:16
  37.5 8.6 %multiply_add_fusion = f32[1,32,16,4,2,256]{5,2,3,1,4,0:T(8,128)S(1)} fusion(bf16[1,47,16,4,2,256]{5,2,3,1,4,0:T(8,128)(2,1)S(1)} %constant_dynamic-update-slice_fusion, f32[16]{0:T(128)S(1)} %get-tuple-element.20, f32[16]{0:T(128)S(1)} %get-tuple-element.21, f32[16]{0:T(128)S(1)} %get-tuple-element.22, f32[16]{0:T(128)S(1)} %get-tuple-element.23, ...), kind=kLoop, calls=%fused_computation.3 | loop fusion | flops 49283072 | bytes 37749760 | tf_op jit(solution)/shard_map/add | solution.py:65
  46.1 2.0 %fusion.6 = f32[32,4,256,16]{2,3,1,0:T(8,128)S(1)} fusion(f32[1,32,16,4,2,256]{5,2,3,1,4,0:T(8,128)S(1)} %multiply_add_fusion), kind=kOutput, calls=%fused_computation.24 | convolution fusion | flops 100666880 | bytes 4194304 | tf_op jit(solution)/shard_map/qk,cmkxn->mcqxn/dot_general | solution.py:71
  48.1 1.9 fusion.9
  50.0 2.0 %fusion.21 = f32[32,4,256,16]{2,3,1,0:T(8,128)S(1)} fusion(f32[32,4,256,16]{2,3,1,0:T(8,128)S(1)} %fusion.9, f32[1,32,16,4,2,256]{5,2,3,1,4,0:T(8,128)S(1)} %multiply_add_fusion), kind=kOutput, calls=%fused_computation.37 | convolution fusion | flops 101191168 | bytes 6291456 | tf_op jit(solution)/shard_map/qk,cmkxn->mcqxn/dot_general | solution.py:68
  52.0 2.6 %fusion.26 = (bf16[32,1,16,4,1,256]{5,2,3,0,4,1:T(8,128)(2,1)S(1)}, bf16[32,1,16,4,1,256]{5,2,3,0,4,1:T(8,128)(2,1)S(1)}) fusion(f32[32,4,256,16]{2,3,1,0:T(8,128)S(1)} %fusion.21, f32[4,256]{1,0:T(4,128)S(1)} %get-tuple-element.37, f32[4,256]{1,0:T(4,128)S(1)} %get-tuple-element.38, f32[32,4,256,16]{2,3,1,0:T(8,128)S(1)} %fusion.6, ...), kind=kOutput, calls=%fused_computation.40 | convolution fusion | flops 105385472 | bytes 8396800 | tf_op jit(solution)/shard_map/qk,cmkxn->mcqxn/dot_general | solution.py:71
  54.9 4.8 %copy.50 = bf16[32,1,16,4,2,256]{5,4,2,0,3,1:T(2,128)(2,1)} copy(bf16[32,1,16,4,2,256]{5,2,3,0,4,1:T(8,128)(2,1)S(1)} %pad_maximum_fusion) | data formatting | bytes 4194304 | tf_op jit(solution)/shard_map/stack | solution.py:78
  59.7 3.2 %reshape.281 = bf16[512,4,512,1]{2,0,1,3:T(8,128)(2,1)S(1)} reshape(bf16[32,1,16,4,2,256]{5,4,2,0,3,1:T(2,128)(2,1)} %copy.50) | data formatting | bytes 4194304 | tf_op jit(solution)/shard_map/convert_element_type | solution.py:78
  64.4 4.4 %fusion.10 = f32[512,256,4]{1,2,0:T(4,128)S(1)} fusion(f32[512,4,256]{2,0,1:T(8,128)S(1)} %get-tuple-element.16), kind=kOutput, calls=%fused_computation.28 | convolution fusion | flops 25166064 | bytes 4194304 | tf_op jit(solution)/shard_map/ec,rcn->ren/dot_general | solution.py:88
  68.8 4.4 %fusion.12 = f32[512,256,4]{1,2,0:T(4,128)S(1)} fusion(f32[512,4,256]{2,0,1:T(8,128)S(1)} %get-tuple-element.16), kind=kOutput, calls=%fused_computation.30 | convolution fusion | flops 25166064 | bytes 4194304 | tf_op jit(solution)/shard_map/ec,rcn->ren/dot_general | solution.py:85
  73.2 4.4 %fusion.14 = f32[512,256,4]{1,2,0:T(4,128)S(1)} fusion(f32[512,4,256]{2,0,1:T(8,128)S(1)} %get-tuple-element.15), kind=kOutput, calls=%fused_computation.32 | convolution fusion | flops 25166064 | bytes 4194304 | tf_op jit(solution)/shard_map/ec,rcn->ren/dot_general | solution.py:88
  77.6 5.5 %fusion.22 = bf16[512,4,256]{2,1,0:T(4,128)(2,1)S(1)} fusion(f32[512,256,4]{1,2,0:T(4,128)S(1)} %fusion.10, f32[512,256,4]{1,2,0:T(4,128)S(1)} %fusion.14, f32[512,256,4]{1,2,0:T(4,128)S(1)} %fusion.12, f32[512,4,256]{2,0,1:T(8,128)S(1)} %get-tuple-element.15), kind=kOutput, calls=%fused_computation.38 | convolution fusion | flops 28311792 | bytes 9437184 | tf_op jit(solution)/shard_map/ec,rcn->ren/dot_general | solution.py:85
  83.9 12.2 %copy.55 = bf16[32,16,1024]{1,0,2:T(8,128)(2,1)} copy(bf16[32,16,1024]{2,1,0:T(8,128)(2,1)S(1)} %reshape.260) | data formatting | bytes 2097152 | tf_op jit(solution)/shard_map/reshape | solution.py:92
  97.6 8.6 %gather_fusion.1 = s32[2048]{0:T(1024)S(1)} fusion(s32[1024]{0:T(1024)S(1)} %copy-done, s32[2048]{0:T(1024)S(1)} %broadcast_clamp_fusion), kind=kCustom, calls=%fused_computation.1 | custom fusion | bytes 24576 | tf_op jit(solution)/shard_map/jit(_take)/gather | solution.py:108
  106.2 8.6 %reduce-scatter.2.cloned.1.call-done = bf16[16,16,1024]{1,0,2:T(8,128)(2,1)} async-done(((bf16[32,16,1024]{1,0,2:T(8,128)(2,1)}), bf16[16,16,1024]{1,0,2:T(8,128)(2,1)}) %reduce-scatter.2.cloned.1.call-update) | async-done | bytes 524304 | tf_op jit(solution)/shard_map/reduce_scatter | solution.py:129
  114.8 18.3 %gather_fusion = bf16[2048,16,16]{2,1,0:T(8,128)(2,1)} fusion(bf16[16,16,1024]{1,0,2:T(8,128)(2,1)} %reduce-scatter.2.cloned.1.call-done, s32[2048]{0:T(1024)S(1)} %broadcast_clamp_fusion), kind=kCustom, calls=%fused_computation | custom fusion | bytes 2105344 | tf_op jit(solution)/shard_map/jit(_take)/gather | solution.py:133
  133.1 12.3 %multiply_bitcast_fusion = bf16[16,16,2048]{1,0,2:T(8,128)(2,1)S(1)} fusion(bf16[2048,16,16]{2,1,0:T(8,128)(2,1)} %gather_fusion, pred[2048]{0:T(1024)(128)(4,1)S(1)} %get-tuple-element.8, bf16[2048]{0:T(1024)(128)(2,1)S(1)} %get-tuple-element.7), kind=kLoop, calls=%fused_computation.2 | loop fusion | flops 1048576 | bytes 2103296 | tf_op jit(solution)/shard_map/mul | solution.py:133
  145.4 3.0 %slice_bitcast_fusion.3 = (bf16[1,16,16,512]{2,1,3,0:T(8,128)(2,1)}, bf16[1,16,16,512]{2,1,3,0:T(8,128)(2,1)}, bf16[1,16,16,512]{2,1,3,0:T(8,128)(2,1)}, bf16[1,16,16,512]{2,1,3,0:T(8,128)(2,1)S(1)}) fusion(bf16[16,16,2048]{1,0,2:T(8,128)(2,1)S(1)} %multiply_bitcast_fusion), kind=kLoop, calls=%fused_computation.7 | loop fusion | bytes 2097152 | tf_op jit(solution)/shard_map/stack | solution.py:135
  148.4 2.5 %copy.56 = bf16[1,16,16,512]{3,2,1,0:T(8,128)(2,1)S(1)} copy(bf16[1,16,16,512]{2,1,3,0:T(8,128)(2,1)} %get-tuple-element.9) | data formatting | bytes 524288 | tf_op jit(solution)/shard_map/stack | solution.py:135
  150.9 2.5 %copy.59 = bf16[1,16,16,512]{3,2,1,0:T(8,128)(2,1)S(1)} copy(bf16[1,16,16,512]{2,1,3,0:T(8,128)(2,1)} %get-tuple-element.10) | data formatting | bytes 524288 | tf_op jit(solution)/shard_map/stack | solution.py:135
  153.4 2.5 %copy.58 = bf16[1,16,16,512]{3,2,1,0:T(8,128)(2,1)S(1)} copy(bf16[1,16,16,512]{2,1,3,0:T(8,128)(2,1)} %get-tuple-element.11) | data formatting | bytes 524288 | tf_op jit(solution)/shard_map/stack | solution.py:135
  157.6 30.8 %all_to_all.5 = bf16[4,16,16,512]{3,2,1,0:T(8,128)(2,1)S(1)} all-to-all(bf16[4,16,16,512]{3,2,1,0:T(8,128)(2,1)S(1)} %pad_maximum_fusion.1), channel_id=1, replica_groups=mesh['grp'=2,'freq'=4,'tm'=2,'pol'=2] {'freq'}, dimensions={0} | all-to-all | bytes 2097152 | tf_op jit(solution)/shard_map/all_to_all | solution.py:135
  (39 shorter events, 12.4 us)
Async XLA Ops:
  6.5 91.0 %copy-start = (s32[1024]{0:T(1024)S(1)}, s32[1024]{0:T(1024)}, u32[]{:S(2)}) copy-start(s32[1024]{0:T(1024)} %param.7) | copy-start | bytes 12292
  6.5 108.3 %reduce-scatter.2.cloned.1.call-start = ((), (), s32[]{:S(2)}) async-start(), calls=%async_computation.2 | async-start | bytes 12582912 | tf_op jit(solution)/shard_map/reduce_scatter | solution.py:129
  8.7 10.5 %copy-start.1 = (f32[1,1,4,2,256]{4,3,2,1,0:T(2,128)S(1)}, f32[1,1,4,2,256]{4,3,2,1,0:T(2,128)}, u32[]{:S(2)}) copy-start(f32[1,1,4,2,256]{4,3,2,1,0:T(2,128)} %param.5) | copy-start | bytes 24580
  9.7 26.2 %collective-permute-start = (bf16[1,15,16,4,2,256]{5,2,3,1,4,0:T(8,128)(2,1)}, bf16[1,15,16,4,2,256]{5,2,3,1,4,0:T(8,128)(2,1)}, u32[]{:S(2)}, u32[]{:S(2)}) collective-permute-start(bf16[1,15,16,4,2,256]{5,2,3,1,4,0:T(8,128)(2,1)} %copy.82), channel_id=1, source_target_pairs={{0,2},{1,3},{4,6},{5,7},{8,10},{9,11},{12,14},{13,15},{16,18},{17,... | collective-permute-start | bytes 2949128 | tf_op jit(solution)/shard_map/ppermute | solution.py:16
  96.1 0.7 copy-start.2
Sparse Core Ops, SparseCore 0:
  96.3 18.4 reduce-scatter.1
